TPU v7x, 512 devices: a whole 4x8x8 slice. The times are simulated.
512 devices in a mesh: row: 16 (over y_lo, x, core), col: 8 (over z), seq: 4 (over y_hi).
Axes of the slice: x: 4, y: 8 (y_hi: 4, y_lo: 2; y = y_hi * 2 + y_lo), z: 8, core: 2. Of those that a mesh axis runs over, the one named last changes fastest.
Arguments:
- left_piece: bfloat16 [512, 32, 1024], P('seq', None, 'row'), may hold values from -6 to 6
- right_piece: bfloat16 [512, 32, 1024], P('seq', 'row', 'col'), may hold values from -6 to 6
- proj_weight: bfloat16 [1024, 128], replicated, may hold values from -4 to 4
- proj_bias: float32 [128], replicated, may hold values from -3 to 3
- pair_rep: bfloat16 [1024, 1024, 128], P(('row', 'seq'), 'col'), may hold values from -6 to 6
- norm_gain: float32 [128], replicated, may hold values from 0.5 to 1.5
- up_weight: bfloat16 [128, 512], replicated, may hold values from -0.5 to 0.5
- up_bias: float32 [512], replicated, may hold values from -3 to 3
- down_weight: bfloat16 [512, 128], replicated, may hold values from -0.25 to 0.25
- down_bias: float32 [128], replicated, may hold values from -3 to 3
Outputs:
- refined: bfloat16 [1024, 1024, 128], P(('row', 'seq'), 'col')
All inputs are finite; a program needn't handle non-finite values.
Results may differ from a plain program's by a relative error of at most 0.0085.
Values may be sent and summed in bfloat16 or wider, within the bound.
A program may use at most 64 MiB of HBM per device.

v0:
```python
import jax
import jax.numpy as jnp
from jax import lax
from jax.sharding import PartitionSpec as P

epsilon = 1e-05


def project_block(row_slab, right_all, proj_weight):
    seq_count, channels, row_count = row_slab.shape
    columns = right_all.shape[2]
    left_mat = row_slab.reshape(seq_count, channels * row_count)
    right_mat = right_all.reshape(seq_count, channels * columns)
    outer_prod = lax.dot_general(
        left_mat, right_mat, (((0,), (0,)), ((), ())), preferred_element_type=jnp.float32
    ).astype(jnp.bfloat16)
    outer_prod = outer_prod.reshape(channels, row_count, channels, columns).transpose(1, 3, 0, 2)
    outer_prod = outer_prod.reshape(row_count * columns, channels * channels)
    result = jnp.dot(outer_prod, proj_weight, preferred_element_type=jnp.float32)
    return result.reshape(row_count, columns, proj_weight.shape[1])


def project_rows(row_slab, right_all, proj_weight):
    seq_count, channels, row_count = row_slab.shape
    sub_rows = 8
    pieces = row_slab.reshape(seq_count, channels, row_count // sub_rows, sub_rows)
    pieces = jnp.moveaxis(pieces, 2, 0)
    result = lax.map(lambda portion: project_block(portion, right_all, proj_weight), pieces)
    return result.reshape(row_count, right_all.shape[2], proj_weight.shape[1])


def transition(middle, norm_gain, up_weight, up_bias, down_weight, down_bias):
    row_count, columns, channels = middle.shape
    values = middle.astype(jnp.float32).reshape(row_count * columns, channels)
    center = jnp.mean(values, axis=1, keepdims=True)
    spread = jnp.mean(jnp.square(values - center), axis=1, keepdims=True)
    normed = ((values - center) * lax.rsqrt(spread + epsilon) * norm_gain).astype(jnp.bfloat16)
    hidden = jnp.maximum(
        jnp.dot(normed, up_weight, preferred_element_type=jnp.float32) + up_bias, 0.0
    ).astype(jnp.bfloat16)
    result = values + jnp.dot(hidden, down_weight, preferred_element_type=jnp.float32) + down_bias
    return result.astype(jnp.bfloat16).reshape(row_count, columns, channels)


def gather_right(right_part):
    return lax.all_gather(right_part, "row", axis=1, tiled=True)


def move_cols(tile):
    return lax.all_to_all(tile, "col", split_axis=0, concat_axis=2, tiled=True)


def on_device(
    left_piece,
    right_piece,
    proj_weight,
    proj_bias,
    pair_rep,
    norm_gain,
    up_weight,
    up_bias,
    down_weight,
    down_bias,
):
    own_rows = pair_rep.shape[0]
    columns = pair_rep.shape[1]
    channels = pair_rep.shape[2]
    groups = lax.axis_size("seq")
    seq_index = lax.axis_index("seq")
    group_len = left_piece.shape[0]
    seq_total = group_len * groups
    left_all, right_seq = (
        lax.all_gather(left_piece, "seq", axis=0, tiled=True),
        lax.all_gather(right_piece, "seq", axis=0, tiled=True),
    )
    right_all = gather_right(right_seq)
    offset = seq_index * own_rows
    summed = jnp.zeros((own_rows, columns, channels), jnp.float32)
    for group_id in range(groups):
        left_group = left_all[group_id * group_len : (group_id + 1) * group_len]
        row_slab = lax.dynamic_slice_in_dim(left_group, offset, own_rows, 2)
        right_group = right_all[group_id * group_len : (group_id + 1) * group_len]
        summed = summed + project_rows(row_slab, right_group, proj_weight)
    update = (summed / seq_total + proj_bias).astype(jnp.bfloat16)
    col_count = lax.axis_size("col")
    rowseq_count = lax.axis_size(("row", "seq"))
    run_len = own_rows // col_count
    section_one = move_cols(update.reshape(col_count, run_len, columns, channels))
    section_two = lax.all_to_all(
        section_one.reshape(run_len, rowseq_count, own_rows, channels),
        ("row", "seq"),
        split_axis=1,
        concat_axis=0,
        tiled=True,
    )
    section_three = move_cols(
        section_two.reshape(col_count, rowseq_count // col_count, 1, run_len, own_rows, channels)
    )
    mirrored = section_three.reshape(columns, own_rows, channels).transpose(1, 0, 2)
    middle = (
        pair_rep.astype(jnp.float32)
        + 0.5 * (update.astype(jnp.float32) + mirrored.astype(jnp.float32))
    ).astype(jnp.bfloat16)
    return transition(middle, norm_gain, up_weight, up_bias, down_weight, down_bias)


def solution(mesh):
    in_specs = (
        P("seq", None, "row"),
        P("seq", "row", "col"),
        P(),
        P(),
        P(("row", "seq"), "col", None),
        P(),
        P(),
        P(),
        P(),
        P(),
    )
    out_specs = P(("row", "seq"), "col", None)
    return jax.shard_map(
        on_device, mesh=mesh, in_specs=in_specs, out_specs=out_specs, check_vma=False
    )
```

profile of v0, /device:TPU:1, one launch (start us, length us, event | category | flops | bytes accessed | tf_op | source)
XLA Modules:
  0.0 234.8 jit_solution(6227691487281684803)
XLA Ops:
  6.5 0.7 all-gather.3.cloned.1.call-update
  7.3 15.7 %all_gather.10 = bf16[512,2,128]{2,1,0:T(2,128)(2,1)S(1)} all-gather(bf16[128,2,128]{2,1,0:T(2,128)(2,1)} %param.19), channel_id=1, replica_groups=mesh['row'=16,'col'=8,'seq'=4] {'seq'}, dimensions={0}, use_global_device_ids=true | all-gather | bytes 327680 | tf_op jit(solution)/shard_map/all_gather | solution.py:74
  23.0 0.7 copy.100
  23.8 43.0 %all-gather.3.cloned.1.call-done = bf16[512,32,64]{0,2,1:T(8,128)(2,1)} async-done(((bf16[128,32,64]{0,2,1:T(8,128)(2,1)}), bf16[512,32,64]{0,2,1:T(8,128)(2,1)}) %all-gather.3.cloned.1.call-update) | async-done | bytes 2097168 | tf_op jit(solution)/shard_map/all_gather | solution.py:73
  66.7 1.8 fusion.68
  68.5 0.7 dynamic-slice_bitcast_fusion.2
  69.2 0.7 dynamic-slice_bitcast_fusion
  69.9 46.1 %all-gather.5.cloned.1.call-done = bf16[512,32,128]{2,0,1:T(8,128)(2,1)} async-done(((bf16[512,2,128]{2,0,1:T(8,128)(2,1)}), bf16[512,32,128]{2,0,1:T(8,128)(2,1)}) %all-gather.5.cloned.1.call-update) | async-done | bytes 4194320 | tf_op jit(solution)/shard_map/all_gather | solution.py:46
  116.0 2.8 %fusion.67 = (bf16[128,32,128]{2,0,1:T(8,128)(2,1)S(1)}, bf16[128,32,128]{2,0,1:T(8,128)(2,1)S(1)}, bf16[128,32,128]{2,0,1:T(8,128)(2,1)S(1)}, bf16[128,32,128]{2,0,1:T(8,128)(2,1)S(1)}) fusion(bf16[512,32,128]{2,0,1:T(8,128)(2,1)} %all-gather.5.cloned.1.call-done), kind=kLoop, calls=%fused_computation.71 | loop fusion | bytes 8388608 | tf_op jit(solution)/shard_map/slice | solution.py:82
  118.8 0.7 copy.104
  119.5 0.7 copy.108
  120.2 0.7 copy.106
  120.9 1.7 copy.102
  122.6 1.1 broadcast.42.clone.2
  123.7 7.8 %while.40 = (s32[]{:T(128)}, f32[2,8,128,128]{3,2,1,0:T(8,128)}, bf16[2,128,32,8]{1,3,0,2:T(8,128)(2,1)}, bf16[128,32,128]{2,1,0:T(8,128)(2,1)}, bf16[1024,128]{1,0:T(8,128)(2,1)}, /*index=5*/s32[]{:T(128)}) while((s32[]{:T(128)}, f32[2,8,128,128]{3,2,1,0:T(8,128)}, bf16[2,128,32,8]{1,3,0,2:T(8,128)(2,1)}, bf16[128,32,128]{2,1,0:T(8,128)(2,1)}, ...), condition=%wide.region_1.2_spmd, body=%wide.region_0.1_spmd.sunk | while | flops 537919488 | bytes 15532201 | solution.py:28
  123.7 2.1 convolution_convert_fusion.8
  125.8 0.8 fusion.96
  126.6 1.0 copy-done.2
  127.6 2.1 convolution_convert_fusion.8
  129.7 0.8 fusion.96
  130.5 1.0 copy-done.2
  131.5 1.1 broadcast.42.clone.1
  132.5 6.9 %while.42 = (s32[]{:T(128)}, f32[2,8,128,128]{3,2,1,0:T(8,128)}, bf16[2,128,32,8]{1,3,0,2:T(8,128)(2,1)}, bf16[128,32,128]{2,1,0:T(8,128)(2,1)S(1)}, bf16[1024,128]{1,0:T(8,128)(2,1)}, /*index=5*/s32[]{:T(128)}) while((s32[]{:T(128)}, f32[2,8,128,128]{3,2,1,0:T(8,128)}, bf16[2,128,32,8]{1,3,0,2:T(8,128)(2,1)}, ...), condition=%wide.region_5.6_spmd, body=%wide.region_4.5_spmd.sunk | while | flops 537919488 | bytes 15532201 | solution.py:28
  132.5 1.7 convolution_convert_fusion.10
  134.2 0.8 fusion.106
  135.0 1.0 copy-done.5
  136.0 1.7 convolution_convert_fusion.10
  137.7 0.8 fusion.106
  138.5 1.0 copy-done.5
  139.6 3.5 %while.43 = (s32[]{:T(128)}, f32[2,8,128,128]{3,2,1,0:T(8,128)S(1)}, bf16[2,128,32,8]{1,3,0,2:T(8,128)(2,1)S(1)}, bf16[128,32,128]{2,1,0:T(8,128)(2,1)S(1)}, bf16[1024,128]{1,0:T(8,128)(2,1)}, /*index=5*/s32[]{:T(128)}) while((s32[]{:T(128)}, f32[2,8,128,128]{3,2,1,0:T(8,128)S(1)}, bf16[2,128,32,8]{1,3,0,2:T(8,128)(2,1)S(1)}, ...), condition=%wide.region_7.8_spmd, body=%wide.region_6.7_spmd.sunk | while | flops 537919488 | bytes 7143537 | solution.py:28
  139.6 0.7 convolution_convert_fusion.11
  140.5 0.8 fusion.111
  141.3 0.8 convolution_convert_fusion.11
  142.3 0.8 fusion.111
  143.2 0.9 copy-done.6
  144.1 3.6 %while.41 = (s32[]{:T(128)}, f32[2,8,128,128]{3,2,1,0:T(8,128)S(1)}, bf16[2,128,32,8]{1,3,0,2:T(8,128)(2,1)S(1)}, bf16[128,32,128]{2,1,0:T(8,128)(2,1)S(1)}, bf16[1024,128]{1,0:T(8,128)(2,1)}, /*index=5*/s32[]{:T(128)}) while((s32[]{:T(128)}, f32[2,8,128,128]{3,2,1,0:T(8,128)S(1)}, bf16[2,128,32,8]{1,3,0,2:T(8,128)(2,1)S(1)}, ...), condition=%wide.region_3.4_spmd, body=%wide.region_2.3_spmd.sunk | while | flops 537919488 | bytes 7143537 | solution.py:28
  144.1 0.7 convolution_convert_fusion.9
  145.1 0.8 fusion.101
  145.9 0.8 convolution_convert_fusion.9
  146.9 0.8 fusion.101
  147.7 1.8 add_multiply_fusion
  149.7 24.2 %all_to_all.39 = bf16[8,2,128,128]{3,2,1,0:T(8,128)(2,1)S(1)} all-to-all(bf16[8,2,128,128]{3,2,1,0:T(8,128)(2,1)S(1)} %add_convert_fusion), channel_id=1, replica_groups=mesh['row'=16,'col'=8,'seq'=4] {'col'}, dimensions={0} | all-to-all | bytes 1048576 | tf_op jit(solution)/shard_map/all_to_all | solution.py:50
  174.0 28.1 %all_to_all.40 = bf16[2,64,16,128]{3,2,0,1:T(8,128)(2,1)S(1)} all-to-all(bf16[2,64,16,128]{3,2,0,1:T(8,128)(2,1)S(1)} %copy.111), channel_id=1, replica_groups=mesh['row'=16,'col'=8,'seq'=4] {'row','seq'}, dimensions={1} | all-to-all | bytes 1048576 | tf_op jit(solution)/shard_map/all_to_all | solution.py:89
  202.1 20.6 %all_to_all.41 = bf16[8,8,1,2,16,128]{5,4,3,1,2,0:T(8,128)(2,1)S(1)} all-to-all(bf16[8,8,1,2,16,128]{5,4,3,1,2,0:T(8,128)(2,1)S(1)} %bitcast.205), channel_id=1, replica_groups=mesh['row'=16,'col'=8,'seq'=4] {'col'}, dimensions={0} | all-to-all | bytes 1048576 | tf_op jit(solution)/shard_map/all_to_all | solution.py:50
  222.8 1.0 fusion.60
  224.5 0.6 multiply_reduce_fusion
  225.2 0.6 fusion.63
  225.9 2.0 fusion.57
  (61 shorter events, 2.2 us)
Async XLA Ops:
  6.5 219.3 %copy-start = (bf16[512,128]{1,0:T(8,128)(2,1)S(1)}, bf16[512,128]{1,0:T(8,128)(2,1)}, u32[]{:S(2)}) copy-start(bf16[512,128]{1,0:T(8,128)(2,1)} %param.26) | copy-start | bytes 393220
  6.5 60.2 %all-gather.3.cloned.1.call-start = ((), (), s32[]{:S(2)}) async-start(), calls=%async_computation.3 | async-start | bytes 2621440 | tf_op jit(solution)/shard_map/all_gather | solution.py:73
  7.3 108.8 %all-gather.5.cloned.1.call-start = ((), (), s32[]{:S(2)}) async-start(), calls=%async_computation.4 | async-start | bytes 4456448 | tf_op jit(solution)/shard_map/all_gather | solution.py:46
  123.7 2.1 copy-start.1
  123.7 2.1 copy-start.10
  126.6 1.0 copy-start.2
  127.6 2.1 copy-start.1
  127.6 2.1 copy-start.10
  130.5 1.0 copy-start.2
  132.5 1.7 copy-start.4
  132.5 1.7 copy-start.11
  135.0 1.0 copy-start.5
  136.0 1.7 copy-start.4
  136.0 1.7 copy-start.11
  138.5 1.0 copy-start.5
  139.6 1.0 copy-start.12
  141.3 1.0 copy-start.12
  143.1 1.0 copy-start.6
  144.1 3.6 %copy-start.3 = (f32[2,8,128,128]{3,2,1,0:T(8,128)S(1)}, f32[2,8,128,128]{3,2,1,0:T(8,128)}, u32[]{:S(2)}) copy-start(f32[2,8,128,128]{3,2,1,0:T(8,128)} %get-tuple-element.113) | copy-start | bytes 3145732
  144.1 1.0 copy-start.13
  145.9 1.0 copy-start.13
  147.7 1.9 copy-start.8
  174.0 48.8 %copy-start.7 = (bf16[16,128,128]{2,1,0:T(8,128)(2,1)S(1)}, bf16[16,128,128]{2,1,0:T(8,128)(2,1)}, u32[]{:S(2)}) copy-start(bf16[16,128,128]{2,1,0:T(8,128)(2,1)} %param.22) | copy-start | bytes 1572868
  223.8 1.4 copy-start.9
  224.2 1.7 copy-start.14
  224.2 1.7 copy-start.15
  224.2 1.7 copy-start.16
Sparse Core Ops, SparseCore 0:
  9.4 57.2 all-gather.2
  68.9 47.1 all-gather.4
where the time goes:
time: 235 us
  waiting for transfers between devices  89.8 us (38%)
  blocking collectives  88.6 us (38%)
  local copies, waits for them, and re-layouts  18.9 us (8%)
  matrix products  18.8 us (8%)
  between operations  13.7 us (6%)
  other arithmetic  4.69 us (2%)
    all_gather x1, waiting for transfers between devices, gather_right(): return lax.all_gather(right_part, 'row', axis=1, tiled=True)  46.1 us
    all_to_all x2, blocking collectives, move_cols(): return lax.all_to_all(tile, 'col', split_axis=0, concat_axis=2, tiled=True)  44.8 us
    all_gather x1, waiting for transfers between devices, on_device(): lax.all_gather(left_piece, 'seq', axis=0, tiled=True)  43 us
    all_to_all x1, blocking collectives, on_device(): lax.all_to_all(section_one.reshape(run_len, rowseq_count, own_rows, chann...  28.1 us
    all_gather x1, blocking collectives, on_device(): lax.all_gather(right_piece, 'seq', axis=0, tiled=True)  15.7 us
    dot_general x8, matrix products, project_block(): lax.dot_general(left_mat, right_mat, (((0,), (0,)), ((), ())), preferred_...  10.5 us
    dot_general x8, matrix products, project_block(): jnp.dot(outer_prod, proj_weight, preferred_element_type=jnp.float32)  6.24 us
    while x32, local copies, waits for them, and re-layouts  4.73 us
  transfers between devices with their start and end apart: 2, of which 2 were waited for; matrix products, arithmetic and copies ran while one was open for 2% of the time, Pallas kernels for 0%

commit v1 on v0

--- a/solution.py
+++ b/solution.py
@@ -4,6 +4,13 @@
 from jax.sharding import PartitionSpec as P
 
 epsilon = 1e-05
+
+
+def gather_over(x, mesh_axis, along):
+    peers = lax.axis_size(mesh_axis)
+    blocks = jnp.stack([x for _ in range(peers)])
+    blocks = lax.all_to_all(blocks, mesh_axis, split_axis=0, concat_axis=0)
+    return jnp.concatenate(blocks, axis=along)
 
 
 def project_block(row_slab, right_all, proj_weight):
@@ -70,7 +77,7 @@
     group_len = left_piece.shape[0]
     seq_total = group_len * groups
     left_all, right_seq = (
-        lax.all_gather(left_piece, "seq", axis=0, tiled=True),
+        gather_over(left_piece, "seq", 0),
         lax.all_gather(right_piece, "seq", axis=0, tiled=True),
     )
     right_all = gather_right(right_seq)

time: 235 us -> 218 us (0.928)
  waiting for transfers between devices: 89.8 us -> 67.3 us
  blocking collectives: 88.6 us -> 92.3 us
  starting transfers between devices: 0.04 us -> 3.69 us
    all_to_all x0 -> x1, waiting for transfers between devices: none -> 53 us  [gather_over(): blocks = lax.all_to_all(blocks, mesh_axis, split_axis=0, concat_axis=0)]
    all_gather x1 -> x0, waiting for transfers between devices: 43 us -> none  [on_device(): lax.all_gather(left_piece, 'seq', axis=0, tiled=True)]
    all_gather x1, waiting for transfers between devices: 46.1 us -> 14.3 us  [gather_right(): return lax.all_gather(right_part, 'row', axis=1, tiled=True)]
    all_to_all x1, blocking collectives: 28.1 us -> 33.4 us  [on_device(): lax.all_to_all(section_one.reshape(run_len, rowseq_count, own_rows, chann...]
    while x32 -> x12, local copies, waits for them, and re-layouts: 4.73 us -> 0.75 us
    all_to_all x0 -> x1, starting transfers between devices: none -> 3.69 us  [gather_over(): blocks = lax.all_to_all(blocks, mesh_axis, split_axis=0, concat_axis=0)]
    while x4, local copies, waits for them, and re-layouts: 3.74 us -> 6.77 us  [project_rows(): lax.map(lambda portion: project_block(portion, right_all, proj_weight), p...]
    dot_general x8, matrix products: 10.5 us -> 7.8 us  [project_block(): lax.dot_general(left_mat, right_mat, (((0,), (0,)), ((), ())), preferred_...]
where the time goes in v1:
time: 218 us
  blocking collectives  92.3 us (42%)
  waiting for transfers between devices  67.3 us (31%)
  local copies, waits for them, and re-layouts  18.2 us (8%)
  matrix products  17.7 us (8%)
  between operations  13.6 us (6%)
  other arithmetic  4.69 us (2%)
  starting transfers between devices  3.69 us (2%)
    all_to_all x1, waiting for transfers between devices, gather_over(): blocks = lax.all_to_all(blocks, mesh_axis, split_axis=0, concat_axis=0)  53 us
    all_to_all x2, blocking collectives, move_cols(): return lax.all_to_all(tile, 'col', split_axis=0, concat_axis=2, tiled=True)  43.1 us
    all_to_all x1, blocking collectives, on_device(): lax.all_to_all(section_one.reshape(run_len, rowseq_count, own_rows, chann...  33.4 us
    all_gather x1, blocking collectives, on_device(): lax.all_gather(right_piece, 'seq', axis=0, tiled=True)  15.8 us
    all_gather x1, waiting for transfers between devices, gather_right(): return lax.all_gather(right_part, 'row', axis=1, tiled=True)  14.3 us
    dot_general x8, matrix products, project_block(): jnp.dot(outer_prod, proj_weight, preferred_element_type=jnp.float32)  7.86 us
    dot_general x8, matrix products, project_block(): lax.dot_general(left_mat, right_mat, (((0,), (0,)), ((), ())), preferred_...  7.8 us
    while x4, local copies, waits for them, and re-layouts, project_rows(): lax.map(lambda portion: project_block(portion, right_all, proj_weight), p...  6.77 us
  transfers between devices with their start and end apart: 2, of which 2 were waited for; matrix products, arithmetic and copies ran while one was open for 2% of the time, Pallas kernels for 0%

profile of v1, /device:TPU:1, one launch (start us, length us, event | category | flops | bytes accessed | tf_op | source)
XLA Modules:
  0.0 217.7 jit_solution(6159018315559840100)
XLA Ops:
  6.5 15.8 %all_gather.6 = bf16[512,2,128]{2,1,0:T(2,128)(2,1)S(1)} all-gather(bf16[128,2,128]{2,1,0:T(2,128)(2,1)} %param.19), channel_id=1, replica_groups=mesh['row'=16,'col'=8,'seq'=4] {'seq'}, dimensions={0}, use_global_device_ids=true | all-gather | bytes 327680 | tf_op jit(solution)/shard_map/all_gather | solution.py:81
  22.3 0.7 copy.101
  23.1 2.9 %stack.2 = bf16[4,128,32,64]{1,3,2,0:T(8,128)(2,1)} broadcast(bf16[128,32,64]{0,2,1:T(8,128)(2,1)} %param.18), dimensions={1,2,3} | broadcast | bytes 2621440 | tf_op jit(solution)/shard_map/stack | solution.py:11
  26.0 3.7 %all-to-all-start = ((bf16[4,128,32,64]{1,3,2,0:T(8,128)(2,1)}), bf16[4,128,32,64]{1,3,2,0:T(8,128)(2,1)S(1)}, u32[]{:S(2)}, u32[]{:S(2)}) async-start(bf16[4,128,32,64]{1,3,2,0:T(8,128)(2,1)} %stack.2), calls=%async_computation | async-start | bytes 4194304 | tf_op jit(solution)/shard_map/all_to_all | solution.py:12
  29.7 53.0 %all-to-all-done = bf16[4,128,32,64]{1,3,2,0:T(8,128)(2,1)S(1)} async-done(((bf16[4,128,32,64]{1,3,2,0:T(8,128)(2,1)}), bf16[4,128,32,64]{1,3,2,0:T(8,128)(2,1)S(1)}, u32[]{:S(2)}, u32[]{:S(2)}) %all-to-all-start) | async-done | bytes 2097184 | tf_op jit(solution)/shard_map/all_to_all | solution.py:12
  82.7 0.2 fusion.68
  82.9 0.7 dynamic-slice_bitcast_fusion.2
  83.6 14.3 %all-gather.2.cloned.1.call-done = bf16[512,32,128]{2,0,1:T(8,128)(2,1)} async-done(((bf16[512,2,128]{2,0,1:T(8,128)(2,1)}), bf16[512,32,128]{2,0,1:T(8,128)(2,1)}) %all-gather.2.cloned.1.call-update) | async-done | bytes 4194320 | tf_op jit(solution)/shard_map/all_gather | solution.py:53
  97.9 4.1 %fusion.67 = (bf16[128,32,128]{2,0,1:T(8,128)(2,1)}, bf16[128,32,128]{2,0,1:T(8,128)(2,1)}, bf16[128,32,128]{2,0,1:T(8,128)(2,1)}, bf16[128,32,128]{2,0,1:T(8,128)(2,1)S(1)}) fusion(bf16[512,32,128]{2,0,1:T(8,128)(2,1)} %all-gather.2.cloned.1.call-done), kind=kLoop, calls=%fused_computation.71 | loop fusion | bytes 8388608 | tf_op jit(solution)/shard_map/slice | solution.py:89
  102.0 0.7 copy.103
  102.8 0.2 copy-done.5
  103.0 3.1 %while.40 = (s32[]{:T(128)}, f32[2,8,128,128]{3,2,1,0:T(8,128)S(1)}, bf16[2,128,32,8]{1,3,0,2:T(8,128)(2,1)S(1)}, bf16[128,32,128]{2,1,0:T(8,128)(2,1)S(1)}, bf16[1024,128]{1,0:T(8,128)(2,1)S(1)}, /*index=5*/s32[]{:T(128)}) while((s32[]{:T(128)}, f32[2,8,128,128]{3,2,1,0:T(8,128)S(1)}, bf16[2,128,32,8]{1,3,0,2:T(8,128)(2,1)S(1)}, ...), condition=%wide.region_1.2_spmd, body=%wide.region_0.1_spmd.sunk | while | flops 537919488 | bytes 6094925 | solution.py:35
  103.0 0.7 convolution_convert_fusion.8
  103.7 0.8 fusion.96
  104.5 0.8 convolution_convert_fusion.8
  105.3 0.8 fusion.96
  106.1 1.9 copy.105
  108.1 4.9 %while.41 = (s32[]{:T(128)}, f32[2,8,128,128]{3,2,1,0:T(8,128)S(1)}, bf16[2,128,32,8]{1,3,0,2:T(8,128)(2,1)}, bf16[128,32,128]{2,1,0:T(8,128)(2,1)S(1)}, bf16[1024,128]{1,0:T(8,128)(2,1)}, /*index=5*/s32[]{:T(128)}) while((s32[]{:T(128)}, f32[2,8,128,128]{3,2,1,0:T(8,128)S(1)}, bf16[2,128,32,8]{1,3,0,2:T(8,128)(2,1)}, ...), condition=%wide.region_3.4_spmd, body=%wide.region_2.3_spmd.sunk | while | flops 537919488 | bytes 7144037 | solution.py:35
  108.1 1.6 convolution_convert_fusion.9
  109.8 0.8 fusion.101
  110.6 1.6 convolution_convert_fusion.9
  112.2 0.8 fusion.101
  113.0 2.3 %copy.107 = bf16[128,32,128]{2,1,0:T(8,128)(2,1)S(1)} copy(bf16[128,32,128]{2,0,1:T(8,128)(2,1)} %get-tuple-element.259) | data formatting | bytes 2097152 | tf_op jit(solution)/shard_map/while | solution.py:35
  115.3 1.1 broadcast.44.clone.1
  116.4 5.1 %while.42 = (s32[]{:T(128)}, f32[2,8,128,128]{3,2,1,0:T(8,128)}, bf16[2,128,32,8]{1,3,0,2:T(8,128)(2,1)S(1)}, bf16[128,32,128]{2,1,0:T(8,128)(2,1)S(1)}, bf16[1024,128]{1,0:T(8,128)(2,1)}, /*index=5*/s32[]{:T(128)}) while((s32[]{:T(128)}, f32[2,8,128,128]{3,2,1,0:T(8,128)}, bf16[2,128,32,8]{1,3,0,2:T(8,128)(2,1)S(1)}, ...), condition=%wide.region_5.6_spmd, body=%wide.region_4.5_spmd.sunk | while | flops 537919488 | bytes 7144037 | solution.py:35
  116.4 0.7 convolution_convert_fusion.10
  117.2 0.2 copy-done.7
  117.4 1.6 fusion.106
  119.0 0.8 convolution_convert_fusion.10
  119.7 0.2 copy-done.7
  119.9 1.6 fusion.106
  121.5 1.9 copy.109
  123.5 3.5 %while.43 = (s32[]{:T(128)}, f32[2,8,128,128]{3,2,1,0:T(8,128)S(1)}, bf16[2,128,32,8]{1,3,0,2:T(8,128)(2,1)S(1)}, bf16[128,32,128]{2,1,0:T(8,128)(2,1)S(1)}, bf16[1024,128]{1,0:T(8,128)(2,1)}, /*index=5*/s32[]{:T(128)}) while((s32[]{:T(128)}, f32[2,8,128,128]{3,2,1,0:T(8,128)S(1)}, bf16[2,128,32,8]{1,3,0,2:T(8,128)(2,1)S(1)}, ...), condition=%wide.region_7.8_spmd, body=%wide.region_6.7_spmd.sunk | while | flops 537919488 | bytes 7143529 | solution.py:35
  123.5 0.7 convolution_convert_fusion.11
  124.3 0.2 copy-done.8
  124.5 0.8 fusion.111
  125.3 0.8 convolution_convert_fusion.11
  126.0 0.2 copy-done.8
  126.2 0.8 fusion.111
  127.0 1.8 add_multiply_fusion
  129.0 22.7 %all_to_all.44 = bf16[8,2,128,128]{3,2,1,0:T(8,128)(2,1)S(1)} all-to-all(bf16[8,2,128,128]{3,2,1,0:T(8,128)(2,1)S(1)} %add_convert_fusion), channel_id=1, replica_groups=mesh['row'=16,'col'=8,'seq'=4] {'col'}, dimensions={0} | all-to-all | bytes 1048576 | tf_op jit(solution)/shard_map/all_to_all | solution.py:57
  151.8 33.4 %all_to_all.45 = bf16[2,64,16,128]{3,2,0,1:T(8,128)(2,1)S(1)} all-to-all(bf16[2,64,16,128]{3,2,0,1:T(8,128)(2,1)S(1)} %copy.112), channel_id=1, replica_groups=mesh['row'=16,'col'=8,'seq'=4] {'row','seq'}, dimensions={1} | all-to-all | bytes 1048576 | tf_op jit(solution)/shard_map/all_to_all | solution.py:96
  185.2 20.4 %all_to_all.46 = bf16[8,8,1,2,16,128]{5,4,3,1,2,0:T(8,128)(2,1)S(1)} all-to-all(bf16[8,8,1,2,16,128]{5,4,3,1,2,0:T(8,128)(2,1)S(1)} %bitcast.205), channel_id=1, replica_groups=mesh['row'=16,'col'=8,'seq'=4] {'col'}, dimensions={0} | all-to-all | bytes 1048576 | tf_op jit(solution)/shard_map/all_to_all | solution.py:57
  205.8 1.0 fusion.60
  206.8 0.3 convert_reduce_fusion
  207.5 0.6 multiply_reduce_fusion
  208.2 0.6 fusion.63
  208.8 2.0 fusion.57
  (41 shorter events, 1.1 us)
Async XLA Ops:
  6.5 202.3 %copy-start = (bf16[512,128]{1,0:T(8,128)(2,1)S(1)}, bf16[512,128]{1,0:T(8,128)(2,1)}, u32[]{:S(2)}) copy-start(bf16[512,128]{1,0:T(8,128)(2,1)} %param.26) | copy-start | bytes 393220
  6.5 91.4 %all-gather.2.cloned.1.call-start = ((), (), s32[]{:S(2)}) async-start(), calls=%async_computation.4 | async-start | bytes 4456448 | tf_op jit(solution)/shard_map/all_gather | solution.py:53
  26.0 56.7 %all-to-all-start = ((bf16[4,128,32,64]{1,3,2,0:T(8,128)(2,1)}), bf16[4,128,32,64]{1,3,2,0:T(8,128)(2,1)S(1)}, u32[]{:S(2)}, u32[]{:S(2)}) async-start(bf16[4,128,32,64]{1,3,2,0:T(8,128)(2,1)} %stack.2), calls=%async_computation | async-start | bytes 4194304 | tf_op jit(solution)/shard_map/all_to_all | solution.py:12
  102.0 0.9 copy-start.5
  108.1 1.6 copy-start.6
  110.6 1.6 copy-start.6
  113.0 3.4 %copy-start.1 = (f32[2,8,128,128]{3,2,1,0:T(8,128)}, f32[2,8,128,128]{3,2,1,0:T(8,128)S(1)}, u32[]{:S(2)}) copy-start(f32[2,8,128,128]{3,2,1,0:T(8,128)S(1)} %get-tuple-element.114) | copy-start | bytes 3145732
  116.4 1.0 copy-start.7
  119.0 0.9 copy-start.7
  123.5 1.0 copy-start.8
  125.3 1.0 copy-start.8
  127.0 1.9 copy-start.3
  151.8 54.0 %copy-start.2 = (bf16[16,128,128]{2,1,0:T(8,128)(2,1)S(1)}, bf16[16,128,128]{2,1,0:T(8,128)(2,1)}, u32[]{:S(2)}) copy-start(bf16[16,128,128]{2,1,0:T(8,128)(2,1)} %param.22) | copy-start | bytes 1572868
  206.8 1.4 copy-start.4
  207.1 1.7 copy-start.9
  207.1 1.7 copy-start.10
  207.2 1.7 copy-start.11
Sparse Core Ops, SparseCore 0:
  23.2 74.6 all-gather.1
